TPU v7x, 32 devices: a whole 2x2x4 slice. The times are simulated.
32 devices in a mesh: pipe: 2 (over core), ctx: 16 (over z, y, x).
Axes of the slice: x: 2, y: 2, z: 4, core: 2. Of those that a mesh axis runs over, the one named last changes fastest.
Arguments:
- states: bfloat16 [2, 2048, 2048], P('pipe', 'ctx'), may hold values from -6 to 6
- norm_gain: float32 [2, 2048], P('pipe'), may hold values from 0.25 to 1.75
- w_in: bfloat16 [2, 2048, 1536], P('pipe', 'ctx'), may hold values from -1 to 1
- w_out: bfloat16 [2, 1024, 2048], P('pipe', 'ctx'), may hold values from -0.1875 to 0.1875
- lengths: int32 [2, 4], replicated, may hold values from 1 to 1024, 2048 in all within a row
Outputs:
- moved: bfloat16 [2, 2048, 2048], P('pipe', 'ctx')
Inputs may be any that keep to these rules, and one draw needn't show every extreme that they name: Each row of lengths lays the responses of one micro-batch end to end over the 2048 positions.
All inputs are finite; a program needn't handle non-finite values.
Results may differ from a plain program's by a relative error of at most 0.0045.
Values may be sent and summed in bfloat16 or wider, within the bound.
No kernel may reach another device: no remote copies, remote signals or barrier semaphores. Data moves between devices by JAX's collectives and lax.ppermute only.
A program may use at most 64 MiB of HBM per device.

v0:
```python
import jax
import jax.numpy as jnp
from jax import lax
from jax.sharding import PartitionSpec as P

HEAD_DIM = 64
HEADS = 16
KV_HEADS = 4
epsilon = 1e-05
rope_base = 500000.0
masked_score = -1e30


def passed_along(value, axis, steps):
    count = lax.axis_size(axis)
    initial, last = (max(0, -steps), min(count, count - steps))
    return lax.ppermute(value, axis, [(source, source + steps) for source in range(initial, last)])


def passed_along_2(value, axis, steps):
    count = lax.axis_size(axis)
    pairs = [(source, (source + steps) % count) for source in range(count)]
    return lax.ppermute(value, axis, pairs)


def locate(doc_lengths, spots):
    doc_ends = jnp.cumsum(doc_lengths)
    segment = jnp.sum((doc_ends[None, :] <= spots[:, None]).astype(jnp.int32), axis=1)
    starts = doc_ends - doc_lengths
    labels = jnp.arange(doc_lengths.shape[0], dtype=jnp.int32)
    first = jnp.sum(jnp.where(segment[:, None] == labels[None, :], starts[None, :], 0), axis=1)
    return (segment, spots - first)


def rotate_pairs(heads_data, position):
    half_dim = heads_data.shape[-1] // 2
    inverse = rope_base ** (-jnp.arange(half_dim, dtype=jnp.float32) * 2.0 / heads_data.shape[-1])
    angles = position.astype(jnp.float32)[:, None] * inverse[None, :]
    cosine = jnp.cos(angles)[:, None, :]
    sine_part = jnp.sin(angles)[:, None, :]
    first_half = heads_data[..., :half_dim]
    second_half = heads_data[..., half_dim:]
    return jnp.concatenate(
        [
            first_half * cosine - second_half * sine_part,
            second_half * cosine + first_half * sine_part,
        ],
        -1,
    )


def body(states, norm_gain, w_in, w_out, lengths):
    section_index = lax.axis_index("pipe")
    ctx_index = lax.axis_index("ctx")
    ctx_count = lax.axis_size("ctx")
    tok_rows = states.shape[1]
    doc_lengths = lax.dynamic_index_in_dim(lengths, section_index, 0, keepdims=False)
    gain = norm_gain[0]
    weight_in = w_in[0]
    weight_out = w_out[0]
    wide = states[0].astype(jnp.float32)
    normed = (wide * lax.rsqrt(jnp.mean(wide * wide, -1, keepdims=True) + epsilon) * gain).astype(
        jnp.bfloat16
    )
    columns = normed
    proj = jnp.dot(
        columns,
        lax.all_gather(weight_in, "ctx", axis=0, tiled=True),
        preferred_element_type=jnp.float32,
    )
    q_width = HEADS * HEAD_DIM
    k_width = KV_HEADS * HEAD_DIM
    group = HEADS // KV_HEADS
    first_spot = ctx_index * tok_rows
    query_spots = first_spot + jnp.arange(tok_rows, dtype=jnp.int32)
    query_seg, position = locate(doc_lengths, query_spots)
    queries = rotate_pairs(proj[:, :q_width].reshape(tok_rows, HEADS, HEAD_DIM), position).astype(
        jnp.bfloat16
    )
    queries = queries.reshape(tok_rows, KV_HEADS, group, HEAD_DIM)
    keys_rot = rotate_pairs(
        proj[:, q_width : q_width + k_width].reshape(tok_rows, KV_HEADS, HEAD_DIM), position
    ).astype(jnp.bfloat16)
    values = proj[:, q_width + k_width :].astype(jnp.bfloat16)
    key_values = jnp.concatenate([keys_rot.reshape(tok_rows, k_width), values], 1)

    def attend_block(carry, portion, offset):
        row_count = portion.shape[0]
        key_spots = offset + jnp.arange(row_count, dtype=jnp.int32)
        key_seg, unused_place = locate(doc_lengths, key_spots)
        allowed = (
            (query_seg[:, None] == key_seg[None, :])
            & (key_spots[None, :] <= query_spots[:, None])
            & (key_spots[None, :] >= 0)
        )

        def update(state):
            running_max, running_sum, accum = state
            key_part = portion[:, :k_width].reshape(row_count, KV_HEADS, HEAD_DIM)
            value_part = portion[:, k_width:].reshape(row_count, KV_HEADS, HEAD_DIM)
            scores = jnp.einsum(
                "tgjd,rgd->gjtr", queries, key_part, preferred_element_type=jnp.float32
            ) * HEAD_DIM ** (-0.5)
            scores = jnp.where(allowed, scores, masked_score)
            new_max = jnp.maximum(running_max, jnp.max(scores, -1))
            rescale = jnp.exp(running_max - new_max)
            probs = jnp.where(allowed, jnp.exp(scores - new_max[..., None]), 0.0)
            new_sum = running_sum * rescale + jnp.sum(probs, -1)
            product = jnp.einsum(
                "gjtr,rgd->gjtd",
                probs.astype(jnp.bfloat16),
                value_part,
                preferred_element_type=jnp.float32,
            )
            return (new_max, new_sum, accum * rescale[..., None] + product)

        return lax.cond(jnp.any(allowed), update, lambda state: state, carry)

    initial = (
        jnp.full((KV_HEADS, group, tok_rows), masked_score, jnp.float32),
        jnp.zeros((KV_HEADS, group, tok_rows), jnp.float32),
        jnp.zeros((KV_HEADS, group, tok_rows, HEAD_DIM), jnp.float32),
    )
    resp_longest = min(1024, 8 * tok_rows, tok_rows * ctx_count // 2)
    reach_count = min(ctx_count - 1, (resp_longest + tok_rows - 2) // tok_rows)
    needed = reach_count + 1
    collected = key_values
    held = 1
    while held < needed:
        taken = min(held, needed - held)
        arrived = passed_along(collected[collected.shape[0] - taken * tok_rows :], "ctx", held)
        collected = jnp.concatenate([arrived, collected], 0)
        held = held + taken
    carry = initial
    portion = collected
    offset = first_spot - (held - 1) * tok_rows
    row_count = portion.shape[0]
    block_rows = min(row_count, 512)
    full_blocks = row_count // block_rows

    def visit_block(block_idx, state):
        sliced = lax.dynamic_slice_in_dim(portion, block_idx * block_rows, block_rows, 0)
        return attend_block(state, sliced, offset + block_idx * block_rows)

    carry = lax.fori_loop(0, full_blocks, visit_block, carry)
    carry = attend_block(
        carry, portion[full_blocks * block_rows :], offset + full_blocks * block_rows
    )
    running_max, running_sum, accum = carry
    attended = (
        (accum / running_sum[..., None])
        .transpose(2, 0, 1, 3)
        .reshape(tok_rows, q_width)
        .astype(jnp.bfloat16)
    )
    columns = attended
    output = jnp.dot(
        columns,
        lax.all_gather(weight_out, "ctx", axis=0, tiled=True),
        preferred_element_type=jnp.float32,
    )
    new_state = (wide + output).astype(jnp.bfloat16)
    passed = passed_along_2(new_state, "pipe", 1)
    return passed[None]


def solution(mesh):
    return jax.shard_map(
        body,
        mesh=mesh,
        in_specs=(
            P("pipe", "ctx", None),
            P("pipe", None),
            P("pipe", "ctx", None),
            P("pipe", "ctx", None),
            P(),
        ),
        out_specs=P("pipe", "ctx", None),
        check_vma=False,
    )
```

profile of v0, /device:TPU:0, one launch (start us, length us, event | category | flops | bytes accessed | tf_op | source)
XLA Modules:
  0.0 203.2 jit_solution(16966979567751797768)
XLA Ops:
  6.5 0.0 all-gather.5.cloned.1.call-start
  6.5 0.7 all-gather.5.cloned.1.call-update
  7.3 0.0 all-gather.7.cloned.1.call-start
  7.3 0.7 all-gather.7.cloned.1.call-update
  8.0 0.7 fusion.52
  8.7 0.2 reduce-window.6
  8.9 0.1 convert_reduce_fusion.1
  9.0 0.7 fusion.41
  9.7 0.1 select_reduce_fusion
  9.8 1.2 fusion.34
  11.0 0.1 multiply_cosine_fusion
  11.1 95.1 %all-gather.5.cloned.1.call-done = bf16[1,2048,1536]{2,1,0:T(8,128)(2,1)} async-done(((bf16[1,128,1536]{2,1,0:T(8,128)(2,1)}), bf16[1,2048,1536]{2,1,0:T(8,128)(2,1)}) %all-gather.5.cloned.1.call-update) | async-done | bytes 6291472 | tf_op jit(solution)/shard_map/all_gather | solution.py:68
  106.3 0.0 copy-start.2
  106.3 4.0 %fusion.24 = f32[128,1536]{1,0:T(8,128)S(1)} fusion(bf16[1,2048,1536]{2,1,0:T(8,128)(2,1)} %all-gather.5.cloned.1.call-done, bf16[1,128,2048]{2,1,0:T(8,128)(2,1)} %param.11, f32[2048]{0:T(1024)} %bitcast.120, f32[128]{0:T(128)S(1)} %add_rsqrt_fusion), kind=kOutput, calls=%fused_computation.34 | convolution fusion | flops 806354944 | bytes 7610880 | tf_op jit(solution)/shard_map/dot_general | solution.py:66
  110.3 0.1 copy.26
  110.5 0.1 copy.27
  110.6 0.7 pad_maximum_fusion.1
  111.2 3.4 %collective-permute-start.1 = (bf16[128,512]{1,0:T(8,128)(2,1)}, bf16[128,512]{1,0:T(8,128)(2,1)S(1)}, u32[]{:S(2)}, u32[]{:S(2)}) collective-permute-start(bf16[128,512]{1,0:T(8,128)(2,1)} %pad_maximum_fusion.1), channel_id=1, source_target_pairs={{0,1},{1,2},{2,3},{3,4},{4,5},{5,6},{6,7},{7,8},{8,9},{9,10},{10,1... | collective-permute-start | bytes 393224 | tf_op jit(solution)/shard_map/ppermute | solution.py:17
  114.6 4.0 %collective-permute-done.1 = bf16[128,512]{1,0:T(8,128)(2,1)S(1)} collective-permute-done((bf16[128,512]{1,0:T(8,128)(2,1)}, bf16[128,512]{1,0:T(8,128)(2,1)S(1)}, u32[]{:S(2)}, u32[]{:S(2)}) %collective-permute-start.1) | collective-permute-done | bytes 131104 | tf_op jit(solution)/shard_map/ppermute | solution.py:17
  118.6 4.8 %collective-permute-start.2 = (bf16[256,512]{1,0:T(8,128)(2,1)S(1)}, bf16[256,512]{1,0:T(8,128)(2,1)S(1)}, u32[]{:S(2)}, u32[]{:S(2)}) collective-permute-start(bf16[256,512]{1,0:T(8,128)(2,1)S(1)} %maximum_maximum_fusion.1), channel_id=1, source_target_pairs={{0,2},{1,3},{2,4},{3,5},{4,6},{5,7},{6,8},{7,9},{8,10},{9,11},{10,... | collective-permute-start | bytes 786440 | tf_op jit(solution)/shard_map/ppermute | solution.py:17
  123.4 1.4 and_and_fusion.1
  124.9 2.4 %collective-permute-done.2 = bf16[256,512]{1,0:T(8,128)(2,1)S(1)} collective-permute-done((bf16[256,512]{1,0:T(8,128)(2,1)S(1)}, bf16[256,512]{1,0:T(8,128)(2,1)S(1)}, u32[]{:S(2)}, u32[]{:S(2)}) %collective-permute-start.2) | collective-permute-done | bytes 262176 | tf_op jit(solution)/shard_map/ppermute | solution.py:17
  127.3 7.6 %collective-permute-start.3 = (bf16[512,512]{1,0:T(8,128)(2,1)S(1)}, bf16[512,512]{1,0:T(8,128)(2,1)S(1)}, u32[]{:S(2)}, u32[]{:S(2)}) collective-permute-start(bf16[512,512]{1,0:T(8,128)(2,1)S(1)} %maximum_maximum_fusion), channel_id=1, source_target_pairs={{0,4},{1,5},{2,6},{3,7},{4,8},{5,9},{6,10},{7,11},{8,12},{9,13},{1... | collective-permute-start | bytes 1572872 | tf_op jit(solution)/shard_map/ppermute | solution.py:17
  135.0 0.0 copy-done.2
  135.0 0.2 broadcast_in_dim.105
  135.9 5.3 %collective-permute-start = (bf16[128,512]{1,0:T(8,128)(2,1)}, bf16[128,512]{1,0:T(8,128)(2,1)}, u32[]{:S(2)}, u32[]{:S(2)}) collective-permute-start(bf16[128,512]{1,0:T(8,128)(2,1)} %pad_maximum_fusion.1), channel_id=1, source_target_pairs={{0,8},{1,9},{2,10},{3,11},{4,12},{5,13},{6,14},{7,15},{16,24},{17,... | collective-permute-start | bytes 393224 | tf_op jit(solution)/shard_map/ppermute | solution.py:17
  141.2 0.2 copy.28
  141.4 0.1 subtract_convert_fusion
  141.5 16.9 %collective-permute-done = bf16[128,512]{1,0:T(8,128)(2,1)} collective-permute-done((bf16[128,512]{1,0:T(8,128)(2,1)}, bf16[128,512]{1,0:T(8,128)(2,1)}, u32[]{:S(2)}, u32[]{:S(2)}) %collective-permute-start) | collective-permute-done | bytes 131104 | tf_op jit(solution)/shard_map/ppermute | solution.py:17
  158.3 1.5 constant_dynamic-update-slice_fusion.4
  159.9 0.0 collective-permute-done.3
  159.9 0.8 constant_dynamic-update-slice_fusion.3
  160.7 0.7 constant_dynamic-update-slice_fusion.2
  161.4 0.7 constant_dynamic-update-slice_fusion.1
  162.1 0.7 constant_dynamic-update-slice_fusion
  162.7 1.7 copy.29
  164.5 0.0 copy-start.1
  164.5 3.7 %while.20 = (s32[]{:T(128)}, f32[4,4,128]{2,1,0:T(4,128)S(1)}, f32[4,4,128]{2,1,0:T(4,128)S(1)}, f32[4,4,128,64]{2,3,1,0:T(8,128)S(1)}, s32[128]{0:T(128)S(1)}, ...) while((s32[]{:T(128)}, f32[4,4,128]{2,1,0:T(4,128)S(1)}, ...), condition=%wide.region_13.14_spmd.clone, body=%wide.region_6.13_spmd.clone.sunk | while | flops 282668160 | bytes 15872853 | solution.py:145
  164.5 0.1 convert_reduce_fusion.3
  164.6 1.0 fusion.54
  166.4 0.1 convert_reduce_fusion.3
  166.5 1.0 fusion.54
  168.2 0.0 copy-start
  168.2 0.0 copy-done.1
  168.2 1.1 conditional.2
  168.2 0.4 fusion.45
  168.6 0.2 fusion.17
  168.8 0.1 copy.30
  169.0 0.4 convolution_add_fusion
  169.3 0.1 divide_convert_fusion
  169.4 21.3 %all-gather.7.cloned.1.call-done = bf16[1,1024,2048]{2,1,0:T(8,128)(2,1)} async-done(((bf16[1,64,2048]{2,1,0:T(8,128)(2,1)}), bf16[1,1024,2048]{2,1,0:T(8,128)(2,1)}) %all-gather.7.cloned.1.call-update) | async-done | bytes 4194320 | tf_op jit(solution)/shard_map/all_gather | solution.py:159
  190.7 0.0 copy-done
  190.7 2.9 %fusion.31 = bf16[128,2048]{1,0:T(8,128)(2,1)S(1)} fusion(bf16[128,1024]{0,1:T(8,128)(2,1)S(1)} %bitcast.103, bf16[1,1024,2048]{2,1,0:T(8,128)(2,1)} %all-gather.7.cloned.1.call-done, bf16[1,128,2048]{2,1,0:T(8,128)(2,1)S(1)} %copy-done), kind=kOutput, calls=%fused_computation.39 | convolution fusion | flops 537657344 | bytes 5505024 | tf_op jit(solution)/shard_map/dot_general | solution.py:157
  193.6 0.1 collective-permute-start.4
  193.7 1.9 collective-permute-done.4
  195.6 0.8 copy.66
  (27 shorter events, 0.3 us)
Async XLA Ops:
  6.5 99.7 %all-gather.5.cloned.1.call-start = ((), (), s32[]{:S(2)}) async-start(), calls=%async_computation | async-start | bytes 6684672 | tf_op jit(solution)/shard_map/all_gather | solution.py:68
  7.3 183.4 %all-gather.7.cloned.1.call-start = ((), (), s32[]{:S(2)}) async-start(), calls=%async_computation.1 | async-start | bytes 4456448 | tf_op jit(solution)/shard_map/all_gather | solution.py:159
  106.3 28.7 %copy-start.2 = (s32[2,4]{1,0:T(2,128)S(1)}, s32[2,4]{1,0:T(2,128)}, u32[]{:S(2)}) copy-start(s32[2,4]{1,0:T(2,128)} %param.15) | copy-start | bytes 100
  111.2 7.4 %collective-permute-start.1 = (bf16[128,512]{1,0:T(8,128)(2,1)}, bf16[128,512]{1,0:T(8,128)(2,1)S(1)}, u32[]{:S(2)}, u32[]{:S(2)}) collective-permute-start(bf16[128,512]{1,0:T(8,128)(2,1)} %pad_maximum_fusion.1), channel_id=1, source_target_pairs={{0,1},{1,2},{2,3},{3,4},{4,5},{5,6},{6,7},{7,8},{8,9},{9,10},{10,1... | collective-permute-start | bytes 393224 | tf_op jit(solution)/shard_map/ppermute | solution.py:17
  118.6 8.6 %collective-permute-start.2 = (bf16[256,512]{1,0:T(8,128)(2,1)S(1)}, bf16[256,512]{1,0:T(8,128)(2,1)S(1)}, u32[]{:S(2)}, u32[]{:S(2)}) collective-permute-start(bf16[256,512]{1,0:T(8,128)(2,1)S(1)} %maximum_maximum_fusion.1), channel_id=1, source_target_pairs={{0,2},{1,3},{2,4},{3,5},{4,6},{5,7},{6,8},{7,9},{8,10},{9,11},{10,... | collective-permute-start | bytes 786440 | tf_op jit(solution)/shard_map/ppermute | solution.py:17
  127.3 32.5 %collective-permute-start.3 = (bf16[512,512]{1,0:T(8,128)(2,1)S(1)}, bf16[512,512]{1,0:T(8,128)(2,1)S(1)}, u32[]{:S(2)}, u32[]{:S(2)}) collective-permute-start(bf16[512,512]{1,0:T(8,128)(2,1)S(1)} %maximum_maximum_fusion), channel_id=1, source_target_pairs={{0,4},{1,5},{2,6},{3,7},{4,8},{5,9},{6,10},{7,11},{8,12},{9,13},{1... | collective-permute-start | bytes 1572872 | tf_op jit(solution)/shard_map/ppermute | solution.py:17
  135.9 22.5 %collective-permute-start = (bf16[128,512]{1,0:T(8,128)(2,1)}, bf16[128,512]{1,0:T(8,128)(2,1)}, u32[]{:S(2)}, u32[]{:S(2)}) collective-permute-start(bf16[128,512]{1,0:T(8,128)(2,1)} %pad_maximum_fusion.1), channel_id=1, source_target_pairs={{0,8},{1,9},{2,10},{3,11},{4,12},{5,13},{6,14},{7,15},{16,24},{17,... | collective-permute-start | bytes 393224 | tf_op jit(solution)/shard_map/ppermute | solution.py:17
  164.5 3.7 %copy-start.1 = (pred[128,128]{0,1:T(8,128)(4,1)S(1)}, pred[128,128]{0,1:T(8,128)(4,1)}, u32[]{:S(2)}) copy-start(pred[128,128]{0,1:T(8,128)(4,1)} %get-tuple-element.457) | copy-start | bytes 49156
  168.2 22.5 %copy-start = (bf16[1,128,2048]{2,1,0:T(8,128)(2,1)S(1)}, bf16[1,128,2048]{2,1,0:T(8,128)(2,1)}, u32[]{:S(2)}) copy-start(bf16[1,128,2048]{2,1,0:T(8,128)(2,1)} %param.11) | copy-start | bytes 1572868
  193.6 2.0 collective-permute-start.4
Sparse Core Ops, SparseCore 0:
  10.1 96.0 all-gather.4
  109.0 81.5 all-gather.6
where the time goes:
time: 204 us; the launch traced here: 203 us
  waiting for transfers between devices  143 us (70%)
  starting transfers between devices  21.1 us (10%)
  between operations  14.4 us (7%)
  other arithmetic  7.99 us (4%)
  matrix products  7.68 us (4%)
  local copies, waits for them, and re-layouts  7.55 us (4%)
    all_gather x1, waiting for transfers between devices, body(): lax.all_gather(weight_in, 'ctx', axis=0, tiled=True)  95.1 us
    ppermute x4, waiting for transfers between devices, passed_along(): lax.ppermute(value, axis, [(source, source + steps) for source in range(i...  23.3 us
    all_gather x1, waiting for transfers between devices, body(): lax.all_gather(weight_out, 'ctx', axis=0, tiled=True)  21.3 us
    ppermute x4, starting transfers between devices, passed_along(): lax.ppermute(value, axis, [(source, source + steps) for source in range(i...  21 us
    unnamed x12, local copies, waits for them, and re-layouts  6.25 us
  transfers between devices with their start and end apart: 7, of which 6 were waited for; matrix products, arithmetic and copies ran while one was open for 10% of the time, Pallas kernels for 0%

commit v1 on v0

--- a/solution.py
+++ b/solution.py
@@ -65,7 +65,9 @@
     columns = normed
     proj = jnp.dot(
         columns,
-        lax.all_gather(weight_in, "ctx", axis=0, tiled=True),
+        jnp.concatenate(
+            lax.all_to_all(jnp.stack([weight_in] * lax.axis_size("ctx")), "ctx", 0, 0), axis=0
+        ),
         preferred_element_type=jnp.float32,
     )
     q_width = HEADS * HEAD_DIM

time: 204 us -> 269 us (1.32)
  the two profiles are of different devices: /device:TPU:0 before, /device:TPU:25 now
where the time goes in v1:
time: 269 us; the launch traced here: 268 us
  waiting for transfers between devices  197 us (73%)
  starting transfers between devices  27.6 us (10%)
  between operations  14.2 us (5%)
  local copies, waits for them, and re-layouts  11.2 us (4%)
  matrix products  9.41 us (3%)
  other arithmetic  7.37 us (3%)
    all_to_all x1, waiting for transfers between devices, body(): lax.all_to_all(jnp.stack([weight_in] * lax.axis_size('ctx')), 'ctx', 0, 0)  169 us
    ppermute x4, waiting for transfers between devices, passed_along(): lax.ppermute(value, axis, [(source, source + steps) for source in range(i...  25.8 us
    ppermute x4, starting transfers between devices, passed_along(): lax.ppermute(value, axis, [(source, source + steps) for source in range(i...  12.2 us
    ppermute x1, starting transfers between devices, passed_along_2(): return lax.ppermute(value, axis, pairs)  8.79 us
    all_to_all x1, starting transfers between devices, body(): lax.all_to_all(jnp.stack([weight_in] * lax.axis_size('ctx')), 'ctx', 0, 0)  6.57 us
    unnamed x12, local copies, waits for them, and re-layouts  6.23 us
  transfers between devices with their start and end apart: 7, of which 5 were waited for; matrix products, arithmetic and copies ran while one was open for 7% of the time, Pallas kernels for 0%

profile of v1, /device:TPU:25, one launch (start us, length us, event | category | flops | bytes accessed | tf_op | source)
XLA Modules:
  0.0 268.1 jit_solution(8056707321220708251)
XLA Ops:
  6.5 4.3 %stack.3 = bf16[16,128,1536]{2,1,0:T(8,128)(2,1)} broadcast(bf16[128,1536]{1,0:T(8,128)(2,1)} %bitcast.117), dimensions={1,2} | broadcast | bytes 6684672 | tf_op jit(solution)/shard_map/stack | solution.py:69
  10.8 0.0 copy-start.2
  10.8 0.0 copy-start
  10.8 0.0 copy-start.1
  10.8 6.6 %all-to-all-start = ((bf16[16,128,1536]{2,1,0:T(8,128)(2,1)}), bf16[16,128,1536]{2,1,0:T(8,128)(2,1)}, u32[]{:S(2)}, u32[]{:S(2)}) async-start(bf16[16,128,1536]{2,1,0:T(8,128)(2,1)} %stack.3), calls=%async_computation | async-start | bytes 12582912 | tf_op jit(solution)/shard_map/all_to_all | solution.py:69
  17.4 0.0 all-gather.3.cloned.1.call-start
  17.4 0.7 all-gather.3.cloned.1.call-update
  18.1 0.0 copy-done.2
  18.1 0.2 reduce-window.6
  18.3 0.1 convert_reduce_fusion.1
  18.4 0.1 select_reduce_fusion
  18.5 0.0 copy-done
  18.5 0.2 fusion.33
  18.7 0.1 multiply_cosine_fusion
  18.9 168.7 %all-to-all-done = bf16[16,128,1536]{2,1,0:T(8,128)(2,1)} async-done(((bf16[16,128,1536]{2,1,0:T(8,128)(2,1)}), bf16[16,128,1536]{2,1,0:T(8,128)(2,1)}, u32[]{:S(2)}, u32[]{:S(2)}) %all-to-all-start) | async-done | bytes 6291488 | tf_op jit(solution)/shard_map/all_to_all | solution.py:69
  187.6 0.0 copy-done.1
  187.6 3.8 %fusion.37 = f32[128,1536]{1,0:T(8,128)S(1)} fusion(bf16[2048,1536]{1,0:T(8,128)(2,1)} %bitcast.19, bf16[1,128,2048]{2,1,0:T(8,128)(2,1)S(1)} %copy-done, f32[2048]{0:T(1024)S(1)} %bitcast.124, f32[128]{0:T(128)S(1)} %add_rsqrt_fusion), kind=kOutput, calls=%fused_computation.45 | convolution fusion | flops 806354944 | bytes 7610880 | tf_op jit(solution)/shard_map/dot_general | solution.py:66
  191.4 0.1 copy.26
  191.6 0.1 copy.27
  191.7 0.6 pad_maximum_fusion.1
  192.3 1.9 collective-permute-start.1
  194.2 8.7 %collective-permute-done.1 = bf16[128,512]{1,0:T(8,128)(2,1)S(1)} collective-permute-done((bf16[128,512]{1,0:T(8,128)(2,1)}, bf16[128,512]{1,0:T(8,128)(2,1)S(1)}, u32[]{:S(2)}, u32[]{:S(2)}) %collective-permute-start.1) | collective-permute-done | bytes 131104 | tf_op jit(solution)/shard_map/ppermute | solution.py:17
  203.0 7.7 %collective-permute-start.2 = (bf16[256,512]{1,0:T(8,128)(2,1)S(1)}, bf16[256,512]{1,0:T(8,128)(2,1)S(1)}, u32[]{:S(2)}, u32[]{:S(2)}) collective-permute-start(bf16[256,512]{1,0:T(8,128)(2,1)S(1)} %maximum_maximum_fusion.1), channel_id=1, source_target_pairs={{0,2},{1,3},{2,4},{3,5},{4,6},{5,7},{6,8},{7,9},{8,10},{9,11},{10,... | collective-permute-start | bytes 786440 | tf_op jit(solution)/shard_map/ppermute | solution.py:17
  210.7 0.7 and_and_fusion.1
  211.4 2.5 collective-permute-done.2
  214.0 0.8 maximum_maximum_fusion
  214.8 1.3 collective-permute-start.3
  216.1 0.2 broadcast_in_dim.105
  216.9 1.3 collective-permute-start
  218.2 0.2 copy.28
  218.4 0.1 subtract_convert_fusion
  218.5 14.6 %collective-permute-done = bf16[128,512]{1,0:T(8,128)(2,1)} collective-permute-done((bf16[128,512]{1,0:T(8,128)(2,1)}, bf16[128,512]{1,0:T(8,128)(2,1)}, u32[]{:S(2)}, u32[]{:S(2)}) %collective-permute-start) | collective-permute-done | bytes 131104 | tf_op jit(solution)/shard_map/ppermute | solution.py:17
  233.1 1.5 constant_dynamic-update-slice_fusion.4
  234.7 0.0 collective-permute-done.3
  234.7 0.8 constant_dynamic-update-slice_fusion.3
  235.5 0.7 constant_dynamic-update-slice_fusion.2
  236.2 0.7 constant_dynamic-update-slice_fusion.1
  236.9 0.7 constant_dynamic-update-slice_fusion
  237.5 1.7 copy.29
  239.3 6.7 %while.20 = (s32[]{:T(128)}, f32[4,4,128]{2,1,0:T(4,128)S(1)}, f32[4,4,128]{2,1,0:T(4,128)S(1)}, f32[4,4,128,64]{2,3,1,0:T(8,128)S(1)}, s32[128]{0:T(128)S(1)}, ...) while((s32[]{:T(128)}, f32[4,4,128]{2,1,0:T(4,128)S(1)}, ...), condition=%wide.region_13.14_spmd.clone, body=%wide.region_6.13_spmd.clone.sunk | while | flops 282668160 | bytes 15872853 | solution.py:147
  239.3 0.1 convert_reduce_fusion.3
  239.4 1.0 fusion.55
  241.2 0.1 convert_reduce_fusion.3
  241.3 1.0 fusion.55
  242.9 3.1 %conditional.5 = ((f32[4,4,128]{2,1,0:T(4,128)S(1)}, f32[4,4,128]{2,1,0:T(4,128)S(1)}, f32[4,4,128,64]{2,3,1,0:T(8,128)S(1)})) conditional(s32[]{:T(128)} %convert_element_type.128, (f32[4,4,128]{2,1,0:T(4,128)S(1)}, f32[4,4,128]{2,1,0:T(4,128)S(1)}, f32[4,4,128,64]{2,3,1,0:T(8,128)S(1)}) %tuple.82, (pred[128,512]{0,1:T(8,128)(4,1)S(1)}, s32[]{:T(128)}, ...), branch_computations={%region_9.9_spmd, %region_10.12_spmd} | conditional | flops 282333184 | bytes 15794262 | solution.py:119
  243.0 0.8 fusion.2
  243.8 1.0 fusion.4
  244.8 1.2 fusion.8
  246.0 1.1 conditional.2
  246.0 0.4 fusion.45
  246.4 0.2 fusion.17
  246.6 0.1 copy.30
  246.8 0.4 convolution_add_fusion
  247.1 0.1 divide_convert_fusion
  247.2 0.0 all-gather.3.cloned.1.call-done
  247.2 2.9 %fusion.29 = bf16[128,2048]{1,0:T(8,128)(2,1)S(1)} fusion(bf16[128,1024]{0,1:T(8,128)(2,1)S(1)} %bitcast.106, bf16[1,1024,2048]{2,1,0:T(8,128)(2,1)} %all-gather.3.cloned.1.call-done, bf16[1,128,2048]{2,1,0:T(8,128)(2,1)S(1)} %copy-done), kind=kOutput, calls=%fused_computation.37 | convolution fusion | flops 537657344 | bytes 5505024 | tf_op jit(solution)/shard_map/dot_general | solution.py:159
  250.2 8.8 %collective-permute-start.4 = (bf16[128,2048]{1,0:T(8,128)(2,1)S(1)}, bf16[128,2048]{1,0:T(8,128)(2,1)S(1)}, u32[]{:S(2)}, u32[]{:S(2)}) collective-permute-start(bf16[128,2048]{1,0:T(8,128)(2,1)S(1)} %fusion.29), channel_id=1, source_target_pairs={{0,16},{16,0},{1,17},{17,1},{2,18},{18,2},{3,19},{19,3},{4,20},{20... | collective-permute-start | bytes 1572872 | tf_op jit(solution)/shard_map/ppermute | solution.py:23
  259.0 1.5 collective-permute-done.4
  260.5 0.8 copy.66
  (31 shorter events, 0.4 us)
Async XLA Ops:
  10.8 7.3 %copy-start.2 = (s32[2,4]{1,0:T(2,128)S(1)}, s32[2,4]{1,0:T(2,128)}, u32[]{:S(2)}) copy-start(s32[2,4]{1,0:T(2,128)} %param.15) | copy-start | bytes 100
  10.8 7.7 %copy-start = (bf16[1,128,2048]{2,1,0:T(8,128)(2,1)S(1)}, bf16[1,128,2048]{2,1,0:T(8,128)(2,1)}, u32[]{:S(2)}) copy-start(bf16[1,128,2048]{2,1,0:T(8,128)(2,1)} %param.11) | copy-start | bytes 1572868
  10.8 176.8 %copy-start.1 = (f32[1,2048]{1,0:T(1,128)S(1)}, f32[1,2048]{1,0:T(1,128)}, u32[]{:S(2)}) copy-start(f32[1,2048]{1,0:T(1,128)} %param.12) | copy-start | bytes 24580
  10.8 176.8 %all-to-all-start = ((bf16[16,128,1536]{2,1,0:T(8,128)(2,1)}), bf16[16,128,1536]{2,1,0:T(8,128)(2,1)}, u32[]{:S(2)}, u32[]{:S(2)}) async-start(bf16[16,128,1536]{2,1,0:T(8,128)(2,1)} %stack.3), calls=%async_computation | async-start | bytes 12582912 | tf_op jit(solution)/shard_map/all_to_all | solution.py:69
  17.4 229.8 %all-gather.3.cloned.1.call-start = ((), (), s32[]{:S(2)}) async-start(), calls=%async_computation.1 | async-start | bytes 4456448 | tf_op jit(solution)/shard_map/all_gather | solution.py:161
  192.3 10.6 %collective-permute-start.1 = (bf16[128,512]{1,0:T(8,128)(2,1)}, bf16[128,512]{1,0:T(8,128)(2,1)S(1)}, u32[]{:S(2)}, u32[]{:S(2)}) collective-permute-start(bf16[128,512]{1,0:T(8,128)(2,1)} %pad_maximum_fusion.1), channel_id=1, source_target_pairs={{0,1},{1,2},{2,3},{3,4},{4,5},{5,6},{6,7},{7,8},{8,9},{9,10},{10,1... | collective-permute-start | bytes 393224 | tf_op jit(solution)/shard_map/ppermute | solution.py:17
  203.0 11.0 %collective-permute-start.2 = (bf16[256,512]{1,0:T(8,128)(2,1)S(1)}, bf16[256,512]{1,0:T(8,128)(2,1)S(1)}, u32[]{:S(2)}, u32[]{:S(2)}) collective-permute-start(bf16[256,512]{1,0:T(8,128)(2,1)S(1)} %maximum_maximum_fusion.1), channel_id=1, source_target_pairs={{0,2},{1,3},{2,4},{3,5},{4,6},{5,7},{6,8},{7,9},{8,10},{9,11},{10,... | collective-permute-start | bytes 786440 | tf_op jit(solution)/shard_map/ppermute | solution.py:17
  214.8 19.9 %collective-permute-start.3 = (bf16[512,512]{1,0:T(8,128)(2,1)}, bf16[512,512]{1,0:T(8,128)(2,1)S(1)}, u32[]{:S(2)}, u32[]{:S(2)}) collective-permute-start(bf16[512,512]{1,0:T(8,128)(2,1)} %maximum_maximum_fusion), channel_id=1, source_target_pairs={{0,4},{1,5},{2,6},{3,7},{4,8},{5,9},{6,10},{7,11},{8,12},{9,13},{1... | collective-permute-start | bytes 1572872 | tf_op jit(solution)/shard_map/ppermute | solution.py:17
  216.9 16.3 %collective-permute-start = (bf16[128,512]{1,0:T(8,128)(2,1)}, bf16[128,512]{1,0:T(8,128)(2,1)}, u32[]{:S(2)}, u32[]{:S(2)}) collective-permute-start(bf16[128,512]{1,0:T(8,128)(2,1)} %pad_maximum_fusion.1), channel_id=1, source_target_pairs={{0,8},{1,9},{2,10},{3,11},{4,12},{5,13},{6,14},{7,15},{16,24},{17,... | collective-permute-start | bytes 393224 | tf_op jit(solution)/shard_map/ppermute | solution.py:17
  250.2 10.3 %collective-permute-start.4 = (bf16[128,2048]{1,0:T(8,128)(2,1)S(1)}, bf16[128,2048]{1,0:T(8,128)(2,1)S(1)}, u32[]{:S(2)}, u32[]{:S(2)}) collective-permute-start(bf16[128,2048]{1,0:T(8,128)(2,1)S(1)} %fusion.29), channel_id=1, source_target_pairs={{0,16},{16,0},{1,17},{17,1},{2,18},{18,2},{3,19},{19,3},{4,20},{20... | collective-permute-start | bytes 1572872 | tf_op jit(solution)/shard_map/ppermute | solution.py:23
Sparse Core Ops, SparseCore 0:
  20.9 164.6 all-gather.2
